TPU v7x, 32 devices: a whole 2x2x4 slice. The times are simulated.
32 devices in a mesh: epoch: 4 (over y, x), strip: 8 (over z, core).
Axes of the slice: x: 2, y: 2, z: 4, core: 2. Of those that a mesh axis runs over, the one named last changes fastest.
Arguments:
- raw_tiles: float32 [4, 96, 256, 512], P('epoch', 'strip'), may hold values from -6 to 6
- tile_kind: int32 [4, 96], P('epoch', 'strip'), may hold values from 0 to 3
- tile_invvar: float32 [4, 96], P('epoch', 'strip'), may hold values from 0.2 to 5
- tile_heights: int32 [4, 8, 12], P('epoch'), may hold values from 1 to 256, 2048 in all within a row
- row_interp: float32 [4, 256, 256], replicated, may hold values from -0.4 to 1.9
- col_interp: float32 [4, 512, 512], replicated, may hold values from -0.4 to 1.9
- psf_profiles: float32 [2, 2, 31], replicated, may hold values from -1 to 1
- psf_poly: float32 [4, 2, 6], replicated, may hold values from -1 to 1
Outputs:
- difference: float32 [4, 2048, 4096], P('epoch', 'strip')
Inputs may be any that keep to these rules, and one draw needn't show every extreme that they name: `tile_heights`: along the last dimension, the heights of one column block's tiles from the top of the patch down; they sum to 2048, and the tallest is exactly 256.
All inputs are finite; a program needn't handle non-finite values.
Results may differ from a plain program's by a relative error of at most 0.0003.
Values sent between devices are 32-bit elements; how exact they have to be, the bound alone decides.
No kernel may reach another device: no remote copies, remote signals or barrier semaphores. Data moves between devices by JAX's collectives and lax.ppermute only.
A program may use at most 128 MiB of HBM per device.

v0:
```python
import jax
import jax.numpy as jnp
from jax import lax
from jax.sharding import PartitionSpec as P

ROWS_DEV = 256
KSIZE = 31
precise = lax.Precision.HIGHEST


def padded_2(value, sides, width):
    for axis, dim in sides:
        count, length = (lax.axis_size(axis), value.shape[dim])
        up = [(i, (i + 1) % count) for i in range(count - 1)]
        down = [(j, i) for i, j in up]
        last = lax.slice_in_dim(value, length - width, length, axis=dim)
        initial = lax.slice_in_dim(value, 0, width, axis=dim)
        before = lax.ppermute(last, axis, up)
        after = lax.ppermute(initial, axis, down)
        value = jnp.concatenate([before, value, after], axis=dim)
    return value


def positions(first_cell, length, extent):
    counter = (first_cell + jnp.arange(length)).astype(jnp.float32)
    return (2.0 * counter + 1.0) / extent - 1.0


def coeff_maps(poly_rows, row_coords, col_coords):
    row_term = row_coords[:, None]
    col_term = col_coords[None, :]
    terms = poly_rows[..., None, None]
    return (
        terms[..., 0, :, :]
        + terms[..., 1, :, :] * row_term
        + terms[..., 2, :, :] * col_term
        + terms[..., 3, :, :] * row_term * row_term
        + terms[..., 4, :, :] * row_term * col_term
        + terms[..., 5, :, :] * col_term * col_term
    )


def row_pass(padded, profiles):
    margin = KSIZE // 2
    rows_out = padded.shape[0] - 2 * margin
    offset = jnp.arange(padded.shape[0])[None, :] - jnp.arange(rows_out)[:, None]
    onehot = (offset[:, :, None] == jnp.arange(KSIZE)[None, None, :]).astype(jnp.float32)
    banded = jnp.einsum("rqi,ki->krq", onehot, profiles[:, 0, :], precision=precise)
    return jnp.einsum("krq,qc->krc", banded, padded, precision=precise)


def col_pass(padded, profiles):
    margin = KSIZE // 2
    basis_count, rows_out, wide_in = padded.shape
    width_out = wide_in - 2 * margin
    block_cols = 128
    block_count = width_out // block_cols
    extended = jnp.pad(padded, ((0, 0), (0, 0), (0, block_cols - 2 * margin)))
    leading = extended[:, :, :width_out].reshape(basis_count, rows_out, block_count, block_cols)
    trailing = extended[:, :, block_cols : block_cols + width_out].reshape(
        basis_count, rows_out, block_count, block_cols
    )
    window = jnp.concatenate([leading, trailing[:, :, :, : 2 * margin]], axis=3)
    offset = jnp.arange(block_cols + 2 * margin)[:, None] - jnp.arange(block_cols)[None, :]
    onehot = (offset[:, :, None] == jnp.arange(KSIZE)[None, None, :]).astype(jnp.float32)
    toeplitz = jnp.einsum("mci,ki->kmc", onehot, profiles[:, 1, :], precision=precise)
    result = jnp.einsum("krnm,kmc->krnc", window, toeplitz, precision=precise)
    return result.reshape(basis_count, rows_out, width_out)


def shards(
    raw_tiles, tile_kind, tile_invvar, tile_heights, row_interp, col_interp, psf_profiles, psf_poly
):
    strips = lax.axis_size("strip")
    strip_index = lax.axis_index("strip")
    tiles_dev = raw_tiles.shape[1]
    tile_rows = raw_tiles.shape[2]
    tile_cols = raw_tiles.shape[3]
    blocks = tile_heights.shape[1]
    per_col = tile_heights.shape[2]
    ncol_all = blocks * tile_cols
    nrow_all = ROWS_DEV * strips
    sources = strips // blocks
    first_tile = strip_index * tiles_dev
    block_index = first_tile // per_col
    column_heights = lax.dynamic_index_in_dim(tile_heights[0], block_index, 0, keepdims=False)
    column_starts = jnp.cumsum(column_heights) - column_heights
    offset_in = first_tile % per_col
    my_heights = lax.dynamic_slice_in_dim(column_heights, offset_in, tiles_dev)
    my_starts = lax.dynamic_slice_in_dim(column_starts, offset_in, tiles_dev)
    live_rows = jnp.arange(tile_rows)[None, :] < my_heights[:, None]
    masked = jnp.where(live_rows[:, :, None], raw_tiles[0], 0.0)
    tile_kinds = tile_kind[0]
    half_warped = jnp.einsum(
        "tij,tjk->tik", jnp.take(row_interp, tile_kinds, axis=0), masked, precision=precise
    )
    warped = jnp.einsum(
        "tik,tlk->til", half_warped, jnp.take(col_interp, tile_kinds, axis=0), precision=precise
    )
    sky_rows = jnp.arange(nrow_all)
    covering = jnp.sum((sky_rows[:, None] >= my_starts[None, :]).astype(jnp.int32), axis=1) - 1
    chosen = jnp.maximum(covering, 0)
    member = chosen[:, None] == jnp.arange(tiles_dev)[None, :]
    start_of = jnp.sum(jnp.where(member, my_starts[None, :], 0), axis=1)
    height_of = jnp.sum(jnp.where(member, my_heights[None, :], 0), axis=1)
    weight_of = jnp.sum(jnp.where(member, tile_invvar[0][None, :], 0.0), axis=1)
    local_row = sky_rows - start_of
    covered = (covering >= 0) & (local_row < height_of)
    source = chosen * tile_rows + jnp.clip(local_row, 0, tile_rows - 1)
    picked = jnp.take(warped.reshape(tiles_dev * tile_rows, tile_cols), source, axis=0)
    outgoing = jnp.where(covered[:, None], picked, 0.0).reshape(strips, ROWS_DEV, tile_cols)
    out_weight = jnp.where(covered, weight_of, 0.0).reshape(strips, ROWS_DEV)
    incoming, in_weight = (
        lax.all_to_all(outgoing, "strip", split_axis=0, concat_axis=0, tiled=True),
        lax.all_to_all(out_weight, "strip", split_axis=0, concat_axis=0, tiled=True),
    )
    gathered = jnp.sum(incoming.reshape(blocks, sources, ROWS_DEV, tile_cols), axis=1)
    weights = jnp.transpose(jnp.sum(in_weight.reshape(blocks, sources, ROWS_DEV), axis=1))
    science_blocks = jnp.transpose(gathered, (1, 0, 2))
    weighted = (science_blocks * weights[:, :, None]).reshape(ROWS_DEV, ncol_all)
    science = science_blocks.reshape(ROWS_DEV, ncol_all)
    row_coords = positions(strip_index * ROWS_DEV, ROWS_DEV, nrow_all)
    epochs = lax.axis_size("epoch")
    share_cols = ncol_all // epochs
    weighted_sum, weight_sum = (
        lax.psum_scatter(weighted, "epoch", scatter_dimension=1, tiled=True),
        lax.psum_scatter(weights, "epoch", scatter_dimension=1, tiled=True),
    )
    template = (
        weighted_sum.reshape(ROWS_DEV, blocks // epochs, tile_cols) / weight_sum[:, :, None]
    ).reshape(ROWS_DEV, share_cols)
    padded = padded_2(template, (("epoch", 1), ("strip", 0)), KSIZE // 2)
    convolved = col_pass(row_pass(padded, psf_profiles), psf_profiles)
    col_coords = positions(lax.axis_index("epoch") * share_cols, share_cols, ncol_all)
    coeffs = coeff_maps(psf_poly, row_coords, col_coords)
    matched = coeffs[:, 0] * convolved[0][None] + coeffs[:, 1] * convolved[1][None]
    returned = lax.all_to_all(matched, "epoch", split_axis=0, concat_axis=2, tiled=True)
    return science[None] - returned


def solution(mesh):
    in_specs = (
        P("epoch", "strip", None, None),
        P("epoch", "strip"),
        P("epoch", "strip"),
        P("epoch", None, None),
        P(),
        P(),
        P(),
        P(),
    )
    out_specs = P("epoch", "strip", None)
    return jax.shard_map(shards, mesh=mesh, in_specs=in_specs, out_specs=out_specs, check_vma=False)
```

profile of v0, /device:TPU:9, one launch (start us, length us, event | category | flops | bytes accessed | tf_op | source)
XLA Modules:
  0.0 344.2 jit_solution(10702041812588887044)
XLA Ops:
  9.9 5.6 %all-to-all-start.1 = ((f32[8,1,256]{2,1,0:T(1,128)}), f32[8,1,256]{2,1,0:T(1,128)S(1)}, u32[]{:S(2)}, u32[]{:S(2)}) async-start(f32[8,1,256]{2,1,0:T(1,128)} %copy.67), calls=%async_computation.1 | async-start | bytes 16384 | tf_op jit(solution)/shard_map/all_to_all | solution.py:115
  17.0 2.4 gather_fusion
  19.4 8.8 %gather_fusion.1 = f32[12,512,512]{2,1,0:T(8,128)} fusion(f32[4,512,512]{2,1,0:T(8,128)} %param.13, s32[1024]{0:T(1024)S(1)} %pad_clamp_fusion), kind=kCustom, calls=%fused_computation.1 | custom fusion | bytes 25165872 | tf_op jit(solution)/shard_map/jit(_take)/gather | solution.py:98
  28.2 8.8 %fusion.3 = f32[12,256,512]{2,1,0:T(8,128)S(1)} fusion(f32[1,12,256,512]{3,2,1,0:T(8,128)} %param.8, f32[12,256,256]{2,1,0:T(8,128)} %gather_fusion, pred[12,256]{1,0:T(8,128)(4,1)S(1)} %iota_compare_fusion.10, pred[12]{0:T(512)(128)(4,1)S(1)} %compare_and_fusion.2), kind=kOutput, calls=%fused_computation.9 | convolution fusion | flops 4834197504 | bytes 15731724 | tf_op jit(solution)/shard_map/tij,tjk->tik/dot_general | solution.py:94
  37.0 15.8 %fusion = f32[12,256,512]{2,1,0:T(8,128)} fusion(f32[12,256,512]{2,1,0:T(8,128)S(1)} %fusion.3, f32[12,512,512]{2,1,0:T(8,128)} %gather_fusion.1, pred[12]{0:T(512)(128)(4,1)S(1)} %compare_and_fusion.2), kind=kOutput, calls=%fused_computation.4 | convolution fusion | flops 9666822144 | bytes 25165836 | tf_op jit(solution)/shard_map/tik,tlk->til/dot_general | solution.py:97
  52.8 12.3 %gather_fusion.2 = f32[2048,512]{1,0:T(8,128)} fusion(f32[3072,512]{1,0:T(8,128)} %bitcast.83, s32[2048]{0:T(1024)S(1)} %broadcast_clamp_fusion), kind=kCustom, calls=%fused_computation.2 | custom fusion | bytes 8396800 | tf_op jit(solution)/shard_map/jit(_take)/gather | solution.py:110
  65.1 4.0 %select_select_fusion = f32[8,256,512]{2,1,0:T(8,128)} fusion(f32[8,256,512]{2,1,0:T(8,128)} %bitcast.86, pred[8,256]{1,0:T(8,128)(4,1)S(1)} %get-tuple-element.18, pred[8,256]{1,0:T(8,128)(4,1)S(1)} %get-tuple-element.17), kind=kLoop, calls=%fused_computation.20 | loop fusion | flops 2097152 | bytes 8392704 | tf_op jit(solution)/shard_map/jit(_where)/select_n | solution.py:111
  69.1 5.1 %all-to-all-start = ((f32[8,256,512]{2,1,0:T(8,128)}), f32[8,256,512]{2,1,0:T(8,128)}, u32[]{:S(2)}, u32[]{:S(2)}) async-start(f32[8,256,512]{2,1,0:T(8,128)} %select_select_fusion), calls=%async_computation | async-start | bytes 8388608 | tf_op jit(solution)/shard_map/all_to_all | solution.py:114
  74.2 90.5 %all-to-all-done = f32[8,256,512]{2,1,0:T(8,128)} async-done(((f32[8,256,512]{2,1,0:T(8,128)}), f32[8,256,512]{2,1,0:T(8,128)}, u32[]{:S(2)}, u32[]{:S(2)}) %all-to-all-start) | async-done | bytes 4194336 | tf_op jit(solution)/shard_map/all_to_all | solution.py:114
  164.7 5.3 %copy.60 = f32[8,256,512]{1,2,0:T(8,128)} copy(f32[8,256,512]{2,1,0:T(8,128)} %all-to-all-done) | data formatting | bytes 8388608 | tf_op jit(solution)/shard_map/all_to_all | solution.py:114
  170.0 4.6 %bitcast_multiply_fusion = f32[256,8,512]{0,2,1:T(8,128)} fusion(f32[8,256,512]{1,2,0:T(8,128)} %copy.60, f32[256,8]{0,1:T(8,128)S(1)} %bitcast.96), kind=kLoop, calls=%fused_computation.19 | loop fusion | flops 1048576 | bytes 8396800 | tf_op jit(solution)/shard_map/mul | solution.py:120
  174.6 5.6 %copy.77 = f32[256,4096]{1,0:T(8,128)} copy(f32[256,4096]{0,1:T(8,128)} %bitcast.87) | data formatting | bytes 8388608 | tf_op jit(solution)/shard_map/reshape | solution.py:120
  183.0 4.8 %fusion.25 = f32[2,256,286]{2,0,1:T(2,128)S(1)} fusion(f32[2,31,1]{1,0,2:T(2,128)S(1)} %bitcast.107, s32[256,286]{1,0:T(8,128)S(1)} %iota_subtract_fusion), kind=kOutput, calls=%fused_computation.39 | convolution fusion | flops 56742400 | bytes 878840 | tf_op jit(solution)/shard_map/rqi,ki->krq/dot_general | solution.py:48
  187.8 4.2 %add_add_fusion = f32[4,2,256,1024]{3,2,0,1:T(8,128)} fusion(f32[4,2,1024]{2,0,1:T(4,128)S(1)} %get-tuple-element.28, f32[1024]{0:T(1024)S(1)} %multiply_add_fusion.1, f32[4,2,256]{2,0,1:T(4,128)S(1)} %get-tuple-element.32, f32[4,2,256]{2,0,1:T(4,128)S(1)} %get-tuple-element.33, f32[4,2,1024]{2,0,1:T(4,128)S(1)} %get-tuple-element.27, ...), kind=kLoop, calls=%fused_computation.7 | loop fusion | flops 10485760 | bytes 8482816 | tf_op jit(solution)/shard_map/add | solution.py:34
  192.0 8.9 %all-reduce.1 = f32[256,8]{0,1:T(8,128)S(1)} all-reduce(f32[256,8]{0,1:T(8,128)S(1)} %bitcast.97), channel_id=3, replica_groups=mesh['epoch'=4,'strip'=8] {'epoch'}, use_global_device_ids=true, to_apply=%region_6.7.clone | all-reduce | flops 2048 | bytes 16384
  201.6 33.4 %reduce-scatter.2.cloned.1.call-done = f32[256,1024]{1,0:T(8,128)} async-done(((f32[256,4096]{1,0:T(8,128)}), f32[256,1024]{1,0:T(8,128)}) %reduce-scatter.2.cloned.1.call-update) | async-done | bytes 1048592 | tf_op jit(solution)/shard_map/reduce_scatter | solution.py:126
  235.1 1.4 div.34
  236.6 3.1 collective-permute-start
  239.7 1.3 collective-permute-start.1
  241.6 5.1 %collective-permute-done.1 = f32[256,15]{1,0:T(8,128)S(1)} collective-permute-done((f32[256,15]{1,0:T(8,128)S(1)}, f32[256,15]{1,0:T(8,128)S(1)}, u32[]{:S(2)}, u32[]{:S(2)}) %collective-permute-start.1) | collective-permute-done | bytes 15392 | tf_op jit(solution)/shard_map/ppermute | solution.py:19
  246.7 0.8 concatenate.9
  247.5 4.4 %collective-permute-start.2 = (f32[15,1054]{1,0:T(8,128)S(1)}, f32[15,1054]{1,0:T(8,128)S(1)}, u32[]{:S(2)}, u32[]{:S(2)}) collective-permute-start(f32[15,1054]{1,0:T(8,128)S(1)} %get-tuple-element.13), channel_id=1, source_target_pairs={{0,1},{1,2},{2,3},{3,4},{4,5},{5,6},{6,7},{8,9},{9,10},{10,11},{11... | collective-permute-start | bytes 189728 | tf_op jit(solution)/shard_map/ppermute | solution.py:18
  251.9 2.1 collective-permute-start.3
  254.1 1.0 fusion.27
  255.1 2.5 collective-permute-done.3
  257.6 3.7 %fusion.20 = f32[2,256,1054]{1,2,0:T(8,128)S(1)} fusion(f32[15,1054]{1,0:T(8,128)S(1)} %collective-permute-done.3, f32[256,1054]{1,0:T(8,128)S(1)} %concatenate.9, f32[15,1054]{1,0:T(8,128)S(1)} %collective-permute-done.2, f32[2,256,286]{2,0,1:T(2,128)S(1)} %fusion.25), kind=kOutput, calls=%fused_computation.34 | convolution fusion | flops 1852674816 | bytes 3950096 | tf_op jit(solution)/shard_map/krq,qc->krc/dot_general | solution.py:49
  261.7 2.3 fusion.13
  264.8 4.7 %fusion.8 = f32[4,256,1024]{2,1,0:T(8,128)S(1)} fusion(f32[4,2,256,1024]{3,2,0,1:T(8,128)} %add_add_fusion, f32[256,1024]{1,0:T(8,128)S(1)} %copy.73, f32[256,1024]{1,0:T(8,128)S(1)} %copy.72), kind=kLoop, calls=%fused_computation.15 | loop fusion | flops 3145728 | bytes 14680064 | tf_op jit(solution)/shard_map/add | solution.py:136
  269.5 50.8 %all_to_all.29 = f32[4,256,1024]{2,1,0:T(8,128)} all-to-all(f32[4,256,1024]{2,1,0:T(8,128)S(1)} %fusion.8), channel_id=1, replica_groups=mesh['epoch'=4,'strip'=8] {'epoch'}, dimensions={0} | all-to-all | bytes 8388608 | tf_op jit(solution)/shard_map/all_to_all | solution.py:137
  320.3 5.4 %copy.74 = f32[4,256,1024]{1,2,0:T(8,128)} copy(f32[4,256,1024]{2,1,0:T(8,128)} %all_to_all.29) | data formatting | bytes 8388608 | tf_op jit(solution)/shard_map/all_to_all | solution.py:137
  325.7 6.1 %bitcast_subtract_fusion = f32[1,256,4096]{1,2,0:T(8,128)} fusion(f32[1,256,4096]{1,2,0:T(8,128)} %bitcast.85, f32[1,256,4096]{1,2,0:T(8,128)} %bitcast.84), kind=kLoop, calls=%fused_computation.18 | loop fusion | flops 1048576 | bytes 12582912 | tf_op jit(solution)/shard_map/sub | solution.py:138
  331.8 5.6 %copy.75 = f32[1,256,4096]{2,1,0:T(8,128)} copy(f32[1,256,4096]{1,2,0:T(8,128)} %bitcast_subtract_fusion) | data formatting | bytes 8388608 | tf_op jit(solution)/shard_map/sub | solution.py:138
  (67 shorter events, 9.5 us)
Async XLA Ops:
  6.5 10.5 %copy-start = (f32[4,256,256]{2,1,0:T(8,128)S(1)}, f32[4,256,256]{2,1,0:T(8,128)}, u32[]{:S(2)}) copy-start(f32[4,256,256]{2,1,0:T(8,128)} %param.12) | copy-start | bytes 3145732
  9.9 59.2 %all-to-all-start.1 = ((f32[8,1,256]{2,1,0:T(1,128)}), f32[8,1,256]{2,1,0:T(1,128)S(1)}, u32[]{:S(2)}, u32[]{:S(2)}) async-start(f32[8,1,256]{2,1,0:T(1,128)} %copy.67), calls=%async_computation.1 | async-start | bytes 16384 | tf_op jit(solution)/shard_map/all_to_all | solution.py:115
  69.1 95.6 %all-to-all-start = ((f32[8,256,512]{2,1,0:T(8,128)}), f32[8,256,512]{2,1,0:T(8,128)}, u32[]{:S(2)}, u32[]{:S(2)}) async-start(f32[8,256,512]{2,1,0:T(8,128)} %select_select_fusion), calls=%async_computation | async-start | bytes 8388608 | tf_op jit(solution)/shard_map/all_to_all | solution.py:114
  74.2 160.9 %reduce-scatter.2.cloned.1.call-start = ((), (), s32[]{:S(2)}) async-start(), calls=%async_computation.4 | async-start | bytes 5242880 | tf_op jit(solution)/shard_map/reduce_scatter | solution.py:126
  180.2 0.7 copy-start.2
  180.2 1.4 copy-start.4
  180.2 2.6 copy-start.3
  236.6 5.0 %collective-permute-start = (f32[256,15]{1,0:T(8,128)S(1)}, f32[256,15]{1,0:T(8,128)S(1)}, u32[]{:S(2)}, u32[]{:S(2)}) collective-permute-start(f32[256,15]{1,0:T(8,128)S(1)} %get-tuple-element.16), channel_id=1, source_target_pairs={{0,8},{8,16},{16,24},{1,9},{9,17},{17,25},{2,10},{10,18},{18,26},{... | collective-permute-start | bytes 46088 | tf_op jit(solution)/shard_map/ppermute | solution.py:18
  239.7 7.0 %collective-permute-start.1 = (f32[256,15]{1,0:T(8,128)S(1)}, f32[256,15]{1,0:T(8,128)S(1)}, u32[]{:S(2)}, u32[]{:S(2)}) collective-permute-start(f32[256,15]{1,0:T(8,128)S(1)} %get-tuple-element.15), channel_id=1, source_target_pairs={{8,0},{16,8},{24,16},{9,1},{17,9},{25,17},{10,2},{18,10},{26,18},{... | collective-permute-start | bytes 46088 | tf_op jit(solution)/shard_map/ppermute | solution.py:19
  247.5 7.5 %collective-permute-start.2 = (f32[15,1054]{1,0:T(8,128)S(1)}, f32[15,1054]{1,0:T(8,128)S(1)}, u32[]{:S(2)}, u32[]{:S(2)}) collective-permute-start(f32[15,1054]{1,0:T(8,128)S(1)} %get-tuple-element.13), channel_id=1, source_target_pairs={{0,1},{1,2},{2,3},{3,4},{4,5},{5,6},{6,7},{8,9},{9,10},{10,11},{11... | collective-permute-start | bytes 189728 | tf_op jit(solution)/shard_map/ppermute | solution.py:18
  251.9 5.7 %collective-permute-start.3 = (f32[15,1054]{1,0:T(8,128)S(1)}, f32[15,1054]{1,0:T(8,128)S(1)}, u32[]{:S(2)}, u32[]{:S(2)}) collective-permute-start(f32[15,1054]{1,0:T(8,128)S(1)} %get-tuple-element.14), channel_id=1, source_target_pairs={{1,0},{2,1},{3,2},{4,3},{5,4},{6,5},{7,6},{9,8},{10,9},{11,10},{12... | collective-permute-start | bytes 189728 | tf_op jit(solution)/shard_map/ppermute | solution.py:19
  325.7 11.7 %copy-start.1 = (f32[4,256,256]{2,1,0:T(8,128)S(1)}, f32[4,256,256]{2,1,0:T(8,128)}, u32[]{:S(2)}) copy-start(f32[4,256,256]{2,1,0:T(8,128)} %param.12) | copy-start | bytes 3145732
Sparse Core Ops, SparseCore 0:
  180.4 54.6 reduce-scatter.1
where the time goes:
time: 345 us; the launch traced here: 344 us
  waiting for transfers between devices  132 us (38%)
  blocking collectives  59.7 us (17%)
  local copies, waits for them, and re-layouts  51.5 us (15%)
  matrix products  36.4 us (11%)
  other arithmetic  28.5 us (8%)
  starting transfers between devices  21.6 us (6%)
  between operations  14.3 us (4%)
    all_to_all x1, waiting for transfers between devices, shards(): lax.all_to_all(outgoing, 'strip', split_axis=0, concat_axis=0, tiled=True)  90.5 us
    all_to_all x1, blocking collectives, shards(): lax.all_to_all(matched, 'epoch', split_axis=0, concat_axis=2, tiled=True)  50.8 us
    reduce_scatter x1, waiting for transfers between devices, shards(): lax.psum_scatter(weighted, 'epoch', scatter_dimension=1, tiled=True)  33.4 us
    dot_general x1, matrix products, shards(): jnp.einsum('tik,tlk->til', half_warped, jnp.take(col_interp, tile_kinds,...  15.8 us
    gather x1, local copies, waits for them, and re-layouts, shards(): jnp.take(warped.reshape(tiles_dev * tile_rows, tile_cols), source, axis=0)  12.3 us
    unnamed x1, blocking collectives  8.89 us
    gather x1, local copies, waits for them, and re-layouts, shards(): jnp.take(col_interp, tile_kinds, axis=0)  8.79 us
    dot_general x1, matrix products, shards(): jnp.einsum('tij,tjk->tik', jnp.take(row_interp, tile_kinds, axis=0), mask...  8.77 us
  transfers between devices with their start and end apart: 7, of which 5 were waited for; matrix products, arithmetic and copies ran while one was open for 19% of the time, Pallas kernels for 0%

commit v1 on v0

--- a/solution.py
+++ b/solution.py
@@ -134,7 +134,9 @@
     col_coords = positions(lax.axis_index("epoch") * share_cols, share_cols, ncol_all)
     coeffs = coeff_maps(psf_poly, row_coords, col_coords)
     matched = coeffs[:, 0] * convolved[0][None] + coeffs[:, 1] * convolved[1][None]
-    returned = lax.all_to_all(matched, "epoch", split_axis=0, concat_axis=2, tiled=True)
+    pieces = jnp.split(matched, lax.axis_size("epoch"), axis=0)
+    arrived = lax.all_to_all(jnp.stack(pieces), "epoch", 0, 0)
+    returned = jnp.concatenate(arrived, axis=2)
     return science[None] - returned
 
 

time: 345 us -> 346 us (level)
  no operation moved by 1% of the time
where the time goes in v1:
time: 346 us; the launch traced here: 345 us
  waiting for transfers between devices  132 us (38%)
  blocking collectives  59.7 us (17%)
  local copies, waits for them, and re-layouts  52.1 us (15%)
  matrix products  36.4 us (11%)
  other arithmetic  29 us (8%)
  starting transfers between devices  21.6 us (6%)
  between operations  14.5 us (4%)
    all_to_all x1, waiting for transfers between devices, shards(): lax.all_to_all(outgoing, 'strip', split_axis=0, concat_axis=0, tiled=True)  90.5 us
    all_to_all x1, blocking collectives, shards(): arrived = lax.all_to_all(jnp.stack(pieces), 'epoch', 0, 0)  50.8 us
    reduce_scatter x1, waiting for transfers between devices, shards(): lax.psum_scatter(weighted, 'epoch', scatter_dimension=1, tiled=True)  33.3 us
    dot_general x1, matrix products, shards(): jnp.einsum('tik,tlk->til', half_warped, jnp.take(col_interp, tile_kinds,...  15.8 us
    gather x1, local copies, waits for them, and re-layouts, shards(): jnp.take(warped.reshape(tiles_dev * tile_rows, tile_cols), source, axis=0)  12.3 us
    unnamed x1, blocking collectives  8.88 us
    gather x1, local copies, waits for them, and re-layouts, shards(): jnp.take(col_interp, tile_kinds, axis=0)  8.78 us
    dot_general x1, matrix products, shards(): jnp.einsum('tij,tjk->tik', jnp.take(row_interp, tile_kinds, axis=0), mask...  8.77 us
  transfers between devices with their start and end apart: 7, of which 5 were waited for; matrix products, arithmetic and copies ran while one was open for 19% of the time, Pallas kernels for 0%

profile of v1, /device:TPU:9, one launch (start us, length us, event | category | flops | bytes accessed | tf_op | source)
XLA Modules:
  0.0 345.2 jit_solution(6730000245482350128)
XLA Ops:
  9.9 5.6 %all-to-all-start.1 = ((f32[8,1,256]{2,1,0:T(1,128)}), f32[8,1,256]{2,1,0:T(1,128)S(1)}, u32[]{:S(2)}, u32[]{:S(2)}) async-start(f32[8,1,256]{2,1,0:T(1,128)} %copy.67), calls=%async_computation.1 | async-start | bytes 16384 | tf_op jit(solution)/shard_map/all_to_all | solution.py:115
  17.0 2.4 gather_fusion
  19.4 8.8 %gather_fusion.1 = f32[12,512,512]{2,1,0:T(8,128)} fusion(f32[4,512,512]{2,1,0:T(8,128)} %param.13, s32[1024]{0:T(1024)S(1)} %pad_clamp_fusion), kind=kCustom, calls=%fused_computation.1 | custom fusion | bytes 25165872 | tf_op jit(solution)/shard_map/jit(_take)/gather | solution.py:98
  28.2 8.8 %fusion.3 = f32[12,256,512]{2,1,0:T(8,128)S(1)} fusion(f32[1,12,256,512]{3,2,1,0:T(8,128)} %param.8, f32[12,256,256]{2,1,0:T(8,128)} %gather_fusion, pred[12,256]{1,0:T(8,128)(4,1)S(1)} %iota_compare_fusion.10, pred[12]{0:T(512)(128)(4,1)S(1)} %compare_and_fusion.2), kind=kOutput, calls=%fused_computation.9 | convolution fusion | flops 4834197504 | bytes 15731724 | tf_op jit(solution)/shard_map/tij,tjk->tik/dot_general | solution.py:94
  37.0 15.8 %fusion = f32[12,256,512]{2,1,0:T(8,128)} fusion(f32[12,256,512]{2,1,0:T(8,128)S(1)} %fusion.3, f32[12,512,512]{2,1,0:T(8,128)} %gather_fusion.1, pred[12]{0:T(512)(128)(4,1)S(1)} %compare_and_fusion.2), kind=kOutput, calls=%fused_computation.4 | convolution fusion | flops 9666822144 | bytes 25165836 | tf_op jit(solution)/shard_map/tik,tlk->til/dot_general | solution.py:97
  52.8 12.3 %gather_fusion.2 = f32[2048,512]{1,0:T(8,128)} fusion(f32[3072,512]{1,0:T(8,128)} %bitcast.88, s32[2048]{0:T(1024)S(1)} %broadcast_clamp_fusion), kind=kCustom, calls=%fused_computation.2 | custom fusion | bytes 8396800 | tf_op jit(solution)/shard_map/jit(_take)/gather | solution.py:110
  65.1 4.0 %select_select_fusion = f32[8,256,512]{2,1,0:T(8,128)} fusion(f32[8,256,512]{2,1,0:T(8,128)} %bitcast.90, pred[8,256]{1,0:T(8,128)(4,1)S(1)} %get-tuple-element.22, pred[8,256]{1,0:T(8,128)(4,1)S(1)} %get-tuple-element.21), kind=kLoop, calls=%fused_computation.21 | loop fusion | flops 2097152 | bytes 8392704 | tf_op jit(solution)/shard_map/jit(_where)/select_n | solution.py:111
  69.1 5.1 %all-to-all-start = ((f32[8,256,512]{2,1,0:T(8,128)}), f32[8,256,512]{2,1,0:T(8,128)}, u32[]{:S(2)}, u32[]{:S(2)}) async-start(f32[8,256,512]{2,1,0:T(8,128)} %select_select_fusion), calls=%async_computation | async-start | bytes 8388608 | tf_op jit(solution)/shard_map/all_to_all | solution.py:114
  74.2 90.5 %all-to-all-done = f32[8,256,512]{2,1,0:T(8,128)} async-done(((f32[8,256,512]{2,1,0:T(8,128)}), f32[8,256,512]{2,1,0:T(8,128)}, u32[]{:S(2)}, u32[]{:S(2)}) %all-to-all-start) | async-done | bytes 4194336 | tf_op jit(solution)/shard_map/all_to_all | solution.py:114
  164.6 5.3 %copy.60 = f32[8,256,512]{1,2,0:T(8,128)} copy(f32[8,256,512]{2,1,0:T(8,128)} %all-to-all-done) | data formatting | bytes 8388608 | tf_op jit(solution)/shard_map/all_to_all | solution.py:114
  170.0 4.6 %bitcast_multiply_fusion = f32[256,8,512]{0,2,1:T(8,128)} fusion(f32[8,256,512]{1,2,0:T(8,128)} %copy.60, f32[256,8]{0,1:T(8,128)S(1)} %bitcast.100), kind=kLoop, calls=%fused_computation.20 | loop fusion | flops 1048576 | bytes 8396800 | tf_op jit(solution)/shard_map/mul | solution.py:120
  174.6 5.6 %copy.77 = f32[256,4096]{1,0:T(8,128)} copy(f32[256,4096]{0,1:T(8,128)} %bitcast.91) | data formatting | bytes 8388608 | tf_op jit(solution)/shard_map/reshape | solution.py:120
  183.2 4.8 %fusion.25 = f32[2,256,286]{2,0,1:T(2,128)S(1)} fusion(f32[2,31,1]{1,0,2:T(2,128)S(1)} %bitcast.111, s32[256,286]{1,0:T(8,128)S(1)} %iota_subtract_fusion), kind=kOutput, calls=%fused_computation.40 | convolution fusion | flops 56742400 | bytes 878840 | tf_op jit(solution)/shard_map/rqi,ki->krq/dot_general | solution.py:48
  188.0 4.2 %add_add_fusion = f32[4,2,256,1024]{3,2,0,1:T(8,128)} fusion(f32[4,2,1024]{2,0,1:T(4,128)S(1)} %get-tuple-element.32, f32[1024]{0:T(1024)S(1)} %multiply_add_fusion.1, f32[4,2,256]{2,0,1:T(4,128)S(1)} %get-tuple-element.36, f32[4,2,256]{2,0,1:T(4,128)S(1)} %get-tuple-element.37, f32[4,2,1024]{2,0,1:T(4,128)S(1)} %get-tuple-element.31, ...), kind=kLoop, calls=%fused_computation.7 | loop fusion | flops 10485760 | bytes 8482816 | tf_op jit(solution)/shard_map/add | solution.py:34
  192.2 8.9 %all-reduce.1 = f32[256,8]{0,1:T(8,128)S(1)} all-reduce(f32[256,8]{0,1:T(8,128)S(1)} %bitcast.101), channel_id=3, replica_groups=mesh['epoch'=4,'strip'=8] {'epoch'}, use_global_device_ids=true, to_apply=%region_6.7.clone | all-reduce | flops 2048 | bytes 16384
  201.8 33.3 %reduce-scatter.2.cloned.1.call-done = f32[256,1024]{1,0:T(8,128)} async-done(((f32[256,4096]{1,0:T(8,128)}), f32[256,1024]{1,0:T(8,128)}) %reduce-scatter.2.cloned.1.call-update) | async-done | bytes 1048592 | tf_op jit(solution)/shard_map/reduce_scatter | solution.py:126
  235.1 1.4 div.34
  236.6 3.1 collective-permute-start
  239.7 1.3 collective-permute-start.1
  241.6 5.1 %collective-permute-done.1 = f32[256,15]{1,0:T(8,128)S(1)} collective-permute-done((f32[256,15]{1,0:T(8,128)S(1)}, f32[256,15]{1,0:T(8,128)S(1)}, u32[]{:S(2)}, u32[]{:S(2)}) %collective-permute-start.1) | collective-permute-done | bytes 15392 | tf_op jit(solution)/shard_map/ppermute | solution.py:19
  246.7 0.8 concatenate.9
  247.5 4.4 %collective-permute-start.2 = (f32[15,1054]{1,0:T(8,128)S(1)}, f32[15,1054]{1,0:T(8,128)S(1)}, u32[]{:S(2)}, u32[]{:S(2)}) collective-permute-start(f32[15,1054]{1,0:T(8,128)S(1)} %get-tuple-element.17), channel_id=1, source_target_pairs={{0,1},{1,2},{2,3},{3,4},{4,5},{5,6},{6,7},{8,9},{9,10},{10,11},{11... | collective-permute-start | bytes 189728 | tf_op jit(solution)/shard_map/ppermute | solution.py:18
  251.9 2.1 collective-permute-start.3
  254.1 1.0 fusion.27
  255.1 2.5 collective-permute-done.3
  257.6 3.7 %fusion.20 = f32[2,256,1054]{1,2,0:T(8,128)S(1)} fusion(f32[15,1054]{1,0:T(8,128)S(1)} %collective-permute-done.3, f32[256,1054]{1,0:T(8,128)S(1)} %concatenate.9, f32[15,1054]{1,0:T(8,128)S(1)} %collective-permute-done.2, f32[2,256,286]{2,0,1:T(2,128)S(1)} %fusion.25), kind=kOutput, calls=%fused_computation.35 | convolution fusion | flops 1852674816 | bytes 3950096 | tf_op jit(solution)/shard_map/krq,qc->krc/dot_general | solution.py:49
  261.7 2.3 fusion.13
  264.8 4.7 %fusion.8 = f32[4,256,1024]{2,1,0:T(8,128)S(1)} fusion(f32[4,2,256,1024]{3,2,0,1:T(8,128)} %add_add_fusion, f32[256,1024]{1,0:T(8,128)S(1)} %copy.73, f32[256,1024]{1,0:T(8,128)S(1)} %copy.72), kind=kLoop, calls=%fused_computation.15 | loop fusion | flops 3145728 | bytes 14680064 | tf_op jit(solution)/shard_map/add | solution.py:136
  270.5 50.8 %all_to_all.16 = f32[4,1,256,1024]{3,2,1,0:T(8,128)} all-to-all(f32[4,1,256,1024]{3,2,1,0:T(8,128)S(1)} %pad_maximum_fusion), channel_id=1, replica_groups=mesh['epoch'=4,'strip'=8] {'epoch'}, dimensions={0} | all-to-all | bytes 8388608 | tf_op jit(solution)/shard_map/all_to_all | solution.py:138
  321.4 5.4 %copy.74 = f32[4,1,256,1024]{2,3,0,1:T(8,128)} copy(f32[4,1,256,1024]{3,2,1,0:T(8,128)} %all_to_all.16) | data formatting | bytes 8388608 | tf_op jit(solution)/shard_map/all_to_all | solution.py:138
  326.7 6.1 %bitcast_subtract_fusion = f32[1,256,4096]{1,2,0:T(8,128)} fusion(f32[4,1,256,1024]{2,3,0,1:T(8,128)} %copy.74, f32[1,256,4096]{1,2,0:T(8,128)} %bitcast.89), kind=kLoop, calls=%fused_computation.19 | loop fusion | flops 1048576 | bytes 12582912 | tf_op jit(solution)/shard_map/sub | solution.py:140
  332.8 5.6 %copy.75 = f32[1,256,4096]{2,1,0:T(8,128)} copy(f32[1,256,4096]{1,2,0:T(8,128)} %bitcast_subtract_fusion) | data formatting | bytes 8388608 | tf_op jit(solution)/shard_map/sub | solution.py:140
  (69 shorter events, 10.6 us)
Async XLA Ops:
  6.5 10.4 %copy-start = (f32[4,256,256]{2,1,0:T(8,128)S(1)}, f32[4,256,256]{2,1,0:T(8,128)}, u32[]{:S(2)}) copy-start(f32[4,256,256]{2,1,0:T(8,128)} %param.12) | copy-start | bytes 3145732
  9.9 59.2 %all-to-all-start.1 = ((f32[8,1,256]{2,1,0:T(1,128)}), f32[8,1,256]{2,1,0:T(1,128)S(1)}, u32[]{:S(2)}, u32[]{:S(2)}) async-start(f32[8,1,256]{2,1,0:T(1,128)} %copy.67), calls=%async_computation.1 | async-start | bytes 16384 | tf_op jit(solution)/shard_map/all_to_all | solution.py:115
  69.1 95.6 %all-to-all-start = ((f32[8,256,512]{2,1,0:T(8,128)}), f32[8,256,512]{2,1,0:T(8,128)}, u32[]{:S(2)}, u32[]{:S(2)}) async-start(f32[8,256,512]{2,1,0:T(8,128)} %select_select_fusion), calls=%async_computation | async-start | bytes 8388608 | tf_op jit(solution)/shard_map/all_to_all | solution.py:114
  74.2 160.9 %reduce-scatter.2.cloned.1.call-start = ((), (), s32[]{:S(2)}) async-start(), calls=%async_computation.4 | async-start | bytes 5242880 | tf_op jit(solution)/shard_map/reduce_scatter | solution.py:126
  180.2 0.7 copy-start.2
  180.2 1.4 copy-start.4
  180.2 2.8 copy-start.3
  236.6 5.0 %collective-permute-start = (f32[256,15]{1,0:T(8,128)S(1)}, f32[256,15]{1,0:T(8,128)S(1)}, u32[]{:S(2)}, u32[]{:S(2)}) collective-permute-start(f32[256,15]{1,0:T(8,128)S(1)} %get-tuple-element.20), channel_id=1, source_target_pairs={{0,8},{8,16},{16,24},{1,9},{9,17},{17,25},{2,10},{10,18},{18,26},{... | collective-permute-start | bytes 46088 | tf_op jit(solution)/shard_map/ppermute | solution.py:18
  239.7 7.0 %collective-permute-start.1 = (f32[256,15]{1,0:T(8,128)S(1)}, f32[256,15]{1,0:T(8,128)S(1)}, u32[]{:S(2)}, u32[]{:S(2)}) collective-permute-start(f32[256,15]{1,0:T(8,128)S(1)} %get-tuple-element.19), channel_id=1, source_target_pairs={{8,0},{16,8},{24,16},{9,1},{17,9},{25,17},{10,2},{18,10},{26,18},{... | collective-permute-start | bytes 46088 | tf_op jit(solution)/shard_map/ppermute | solution.py:19
  247.5 7.6 %collective-permute-start.2 = (f32[15,1054]{1,0:T(8,128)S(1)}, f32[15,1054]{1,0:T(8,128)S(1)}, u32[]{:S(2)}, u32[]{:S(2)}) collective-permute-start(f32[15,1054]{1,0:T(8,128)S(1)} %get-tuple-element.17), channel_id=1, source_target_pairs={{0,1},{1,2},{2,3},{3,4},{4,5},{5,6},{6,7},{8,9},{9,10},{10,11},{11... | collective-permute-start | bytes 189728 | tf_op jit(solution)/shard_map/ppermute | solution.py:18
  251.9 5.7 %collective-permute-start.3 = (f32[15,1054]{1,0:T(8,128)S(1)}, f32[15,1054]{1,0:T(8,128)S(1)}, u32[]{:S(2)}, u32[]{:S(2)}) collective-permute-start(f32[15,1054]{1,0:T(8,128)S(1)} %get-tuple-element.18), channel_id=1, source_target_pairs={{1,0},{2,1},{3,2},{4,3},{5,4},{6,5},{7,6},{9,8},{10,9},{11,10},{12... | collective-permute-start | bytes 189728 | tf_op jit(solution)/shard_map/ppermute | solution.py:19
  326.7 11.7 %copy-start.1 = (f32[4,256,256]{2,1,0:T(8,128)S(1)}, f32[4,256,256]{2,1,0:T(8,128)}, u32[]{:S(2)}) copy-start(f32[4,256,256]{2,1,0:T(8,128)} %param.12) | copy-start | bytes 3145732
Sparse Core Ops, SparseCore 0:
  180.3 54.6 reduce-scatter.1
